TPU v7x, 256 devices: a whole 4x4x8 slice. The times are simulated.
256 devices in a mesh: vert: 16 (over x, z_hi), tm: 16 (over y, z_lo, core).
Axes of the slice: x: 4, y: 4, z: 8 (z_hi: 4, z_lo: 2; z = z_hi * 2 + z_lo), core: 2. Of those that a mesh axis runs over, the one named last changes fastest.
Arguments:
- source: bfloat16 [20480, 2048], P('vert', 'tm'), may hold values from -6 to 6
- band_taps: bfloat16 [2, 2, 65], replicated, may hold values from -0.75 to 0.75
- smooth_taps: bfloat16 [2, 65], replicated, may hold values from 0.0009 to 0.031
- parcel_ids: int32 [3, 20480], P(None, 'vert'), may hold values from 0 to 999, as said below
Outputs:
- envelope_coupling: float32 [16, 2, 1504, 1504], P('tm', None, 'vert')
Inputs may be any that keep to these rules, and one draw needn't show every extreme that they name: `parcel_ids`: row r = 0, 1, 2 gives each vertex's parcel in the atlas of 100, 400 or 1000 parcels (values below that count); every parcel of each atlas has at least one vertex.
All inputs are finite; a program needn't handle non-finite values.
Results may differ from a plain program's by a relative error of at most 0.0053.
Values may be sent and summed in bfloat16 or wider, within the bound.
A program may use at most 64 MiB of HBM per device.

v0:
```python
from functools import partial
import math
import jax
import jax.numpy as jnp
from jax import lax
from jax.sharding import PartitionSpec as P

P1 = 100
P2 = 400
P3 = 1000
BANDS = 2
TAPS = 65
HALF = 32
LAG = 64
LAG_STEP = 1
NLAG = 129
EPSILON = 1e-05


def extended_2(cells, sides, width):
    for axis, dim in sides:
        count = lax.axis_size(axis)
        ends = count - 1
        head = lax.slice_in_dim(cells, 0, width, axis=dim)
        tail = lax.slice_in_dim(cells, cells.shape[dim] - width, cells.shape[dim], axis=dim)
        cells = jnp.concatenate(
            [
                lax.ppermute(tail, axis, [(i, (i + 1) % count) for i in range(ends)]),
                cells,
                lax.ppermute(head, axis, [((i + 1) % count, i) for i in range(ends)]),
            ],
            axis=dim,
        )
    return cells


def toeplitz_band(taps, n_out, n_in):
    period = jnp.concatenate([taps, jnp.zeros((n_in + 1 - taps.shape[0],), taps.dtype)])
    return jnp.tile(period, n_out)[: n_out * n_in].reshape(n_out, n_in)


def resolution_of(parcel):
    first = (parcel >= P1).astype(jnp.int32)
    second = (parcel >= P1 + P2).astype(jnp.int32)
    third = (parcel >= P1 + P2 + P3).astype(jnp.int32)
    return first + second + third


def centered_rows(extended, length):
    level_mean = jnp.mean(extended[:, :, LAG : LAG + length], axis=2, keepdims=True)
    centered = (extended - level_mean).astype(jnp.bfloat16)
    middle = centered[:, :, LAG : LAG + length]
    middle_wide = middle.astype(jnp.float32)
    spread = lax.rsqrt(jnp.mean(middle_wide * middle_wide, axis=2) + EPSILON)
    return (centered, middle, spread)


def make_fold(own_middle, own_spread, owner_start, par_dev, t_dev):
    kernel = own_middle.transpose(1, 0, 2).reshape(BANDS * par_dev, 1, t_dev)
    own_level = resolution_of(owner_start + lax.iota(jnp.int32, par_dev))

    def block_value(visiting, first):
        vis_middle = visiting[:, :, LAG : LAG + t_dev].astype(jnp.float32)
        vis_spread = lax.rsqrt(jnp.mean(vis_middle * vis_middle, axis=2) + EPSILON)
        inner = lax.conv_general_dilated(
            visiting,
            kernel,
            (LAG_STEP,),
            "VALID",
            dimension_numbers=("NCH", "OIH", "NCH"),
            feature_group_count=BANDS,
            preferred_element_type=jnp.float32,
        )
        inner = inner.reshape(par_dev, BANDS, par_dev, NLAG)
        energy = jnp.sum(inner * inner, axis=3).transpose(1, 2, 0)
        scale = own_spread.T[:, :, None] * vis_spread.T[:, None, :] / t_dev
        vis_level = resolution_of(first + lax.iota(jnp.int32, par_dev))
        same = ((own_level[:, None] == vis_level[None, :]) & (own_level[:, None] < 3)).astype(
            jnp.float32
        )
        return energy * scale * scale * same[None] / NLAG

    def guarded(visiting, first):
        result = block_value(visiting, first)
        return result

    def fold_rows(carry, piece, start):
        count = piece.shape[0] // par_dev

        def add_block(block_idx, total):
            first = block_idx * par_dev
            visiting = lax.dynamic_slice_in_dim(piece, block_idx * par_dev, par_dev, 0)
            slot = first // par_dev
            zero = jnp.int32(0)
            return lax.dynamic_update_slice(
                total, guarded(visiting, first)[None], (slot, zero, zero, zero)
            )

        return lax.fori_loop(0, count, add_block, carry)

    return fold_rows


def local(source, band_taps, smooth_taps, parcel_ids):
    vert_dev, t_dev = source.shape
    owners = lax.axis_size("vert")
    total_par = (P1 + P2 + P3 + owners - 1) // owners * owners
    par_dev = total_par // owners
    n_mid = t_dev + 2 * HALF
    n_in = t_dev + 4 * HALF
    first_rows = jax.vmap(partial(toeplitz_band, n_out=n_mid, n_in=n_in))(
        band_taps.reshape(2 * BANDS, TAPS)
    )
    first_mat = first_rows.transpose(2, 0, 1).reshape(n_in, 2 * BANDS * n_mid)
    second_rows = jax.vmap(partial(toeplitz_band, n_out=t_dev, n_in=n_mid))(smooth_taps)
    second_mat = second_rows.transpose(0, 2, 1)
    widened = extended_2(source, (("tm", 1),), 2 * HALF)
    block_rows = math.gcd(vert_dev, 128)

    def filter_block(block):
        wave = jnp.dot(block, first_mat, preferred_element_type=jnp.float32).reshape(
            block_rows, 2, BANDS, n_mid
        )
        power = (wave[:, 0] * wave[:, 0] + wave[:, 1] * wave[:, 1]).astype(jnp.bfloat16)
        return jnp.einsum(
            "vbu,but->vbt", power, second_mat, preferred_element_type=jnp.float32
        ).astype(jnp.bfloat16)

    envelope = lax.map(filter_block, widened.reshape(vert_dev // block_rows, block_rows, n_in))
    flat_env = envelope.reshape(vert_dev, BANDS * t_dev)
    offsets = jnp.array([0, P1, P1 + P2], dtype=jnp.int32)
    global_ids = parcel_ids + offsets[:, None]
    owner_start = lax.axis_index("vert") * par_dev
    empty = jnp.zeros((owners, BANDS, par_dev, par_dev), jnp.float32)

    def one_block(block_idx):
        wanted = block_idx * par_dev + lax.iota(jnp.int32, par_dev)
        hits = jnp.sum(
            (global_ids[:, None, :] == wanted[None, :, None]).astype(jnp.bfloat16), axis=0
        )
        return jnp.dot(hits, flat_env, preferred_element_type=jnp.float32)

    pooled = lax.map(
        one_block, jnp.arange(par_dev * lax.axis_size("vert") // par_dev, dtype=jnp.int32)
    )
    own_sums = lax.psum_scatter(
        pooled.reshape(par_dev * lax.axis_size("vert"), BANDS * t_dev),
        "vert",
        scatter_dimension=0,
        tiled=True,
    )
    own_env = own_sums.reshape(par_dev, BANDS, t_dev)
    own_ext = extended_2(own_env, (("tm", 2),), LAG)
    centered, own_middle, own_spread = centered_rows(own_ext, t_dev)
    fold_rows = make_fold(own_middle, own_spread, owner_start, par_dev, t_dev)
    blocks = fold_rows(empty, lax.all_gather(centered, "vert", axis=0, tiled=True), jnp.int32(0))
    coupling = blocks.transpose(1, 2, 0, 3).reshape(BANDS, par_dev, total_par)
    return coupling[None]


def solution(mesh):
    return jax.shard_map(
        local,
        mesh=mesh,
        in_specs=(P("vert", "tm"), P(), P(), P(None, "vert")),
        out_specs=P("tm", None, "vert", None),
        check_vma=False,
    )
```

profile of v0, /device:TPU:1, one launch (start us, length us, event | category | flops | bytes accessed | tf_op | source)
XLA Modules:
  0.0 328.1 jit_solution(10390628284923040536)
XLA Ops:
  6.5 2.0 fusion.27
  8.5 4.9 %collective-permute-start = (bf16[1280,64]{1,0:T(8,128)(2,1)}, bf16[1280,64]{1,0:T(8,128)(2,1)}, u32[]{:S(2)}, u32[]{:S(2)}) collective-permute-start(bf16[1280,64]{1,0:T(8,128)(2,1)} %get-tuple-element.348), channel_id=1, source_target_pairs={{0,1},{1,2},{2,3},{3,4},{4,5},{5,6},{6,7},{7,8},{8,9},{9,10},{10,1... | collective-permute-start | bytes 491528 | tf_op jit(solution)/shard_map/ppermute | solution.py:28
  13.4 2.2 collective-permute-start.1
  19.1 3.4 %collective-permute-done.1 = bf16[1280,64]{1,0:T(8,128)(2,1)} collective-permute-done((bf16[1280,64]{1,0:T(8,128)(2,1)S(1)}, bf16[1280,64]{1,0:T(8,128)(2,1)}, u32[]{:S(2)}, u32[]{:S(2)}) %collective-permute-start.1) | collective-permute-done | bytes 163872 | tf_op jit(solution)/shard_map/ppermute | solution.py:30
  22.5 1.5 pad_maximum_fusion
  24.0 12.1 %while.38 = (s32[]{:T(128)}, bf16[10,128,2,128]{3,2,1,0:T(2,128)(2,1)}, bf16[10,128,256]{2,1,0:T(8,128)(2,1)S(1)}, bf16[256,768]{0,1:T(8,128)(2,1)S(1)}, bf16[2,192,128]{2,1,0:T(8,128)(2,1)S(1)}, /*index=5*/s32[]{:T(128)}) while((s32[]{:T(128)}, bf16[10,128,2,128]{3,2,1,0:T(2,128)(2,1)}, bf16[10,128,256]{2,1,0:T(8,128)(2,1)S(1)}, ...), condition=%wide.region_1.2_spmd, body=%wide.region_0.1_spmd.sunk | while | flops 63143936 | bytes 1540681 | solution.py:129
  36.1 1.2 copy.58
  37.3 27.9 %while.39 = (s32[]{:T(128)}, f32[16,94,256]{2,1,0:T(8,128)S(1)}, s32[3,1280]{1,0:T(4,128)S(1)}, s32[16]{0:T(128)S(1)}, bf16[1280,256]{1,0:T(8,128)(2,1)S(1)}, /*index=5*/s32[]{:T(128)}, s32[1]{0:T(128)}) while((s32[]{:T(128)}, f32[16,94,256]{2,1,0:T(8,128)S(1)}, s32[3,1280]{1,0:T(4,128)S(1)}, s32[16]{0:T(128)S(1)}, ...), condition=%wide.region_4.5_spmd, body=%wide.region_2.4_spmd.sunk | while | flops 62566496 | bytes 1256285 | solution.py:143
  65.3 55.7 %fusion.2 = f32[96,256]{1,0:T(8,128)S(1)} fusion(f32[1504,256]{1,0:T(8,128)S(1)} %reshape.143), kind=kCustom, calls=%all-reduce-scatter | all-reduce-scatter fusion | flops 393217 | bytes 1639424
  121.1 1.9 collective-permute-start.4
  124.7 7.9 %collective-permute-start.2 = (f32[94,2,64]{2,1,0:T(2,128)S(1)}, f32[94,2,64]{2,1,0:T(2,128)S(1)}, u32[]{:S(2)}, u32[]{:S(2)}) collective-permute-start(f32[94,2,64]{2,1,0:T(2,128)S(1)} %get-tuple-element.350), channel_id=1, source_target_pairs={{0,1},{1,2},{2,3},{3,4},{4,5},{5,6},{6,7},{7,8},{8,9},{9,10},{10,1... | collective-permute-start | bytes 144392 | tf_op jit(solution)/shard_map/ppermute | solution.py:28
  132.7 2.1 collective-permute-start.3
  135.0 3.6 %collective-permute-done.3 = f32[94,2,64]{2,1,0:T(2,128)S(1)} collective-permute-done((f32[94,2,64]{2,1,0:T(2,128)S(1)}, f32[94,2,64]{2,1,0:T(2,128)S(1)}, u32[]{:S(2)}, u32[]{:S(2)}) %collective-permute-start.3) | collective-permute-done | bytes 48160 | tf_op jit(solution)/shard_map/ppermute | solution.py:30
  138.6 1.1 fusion.26
  139.7 1.0 slice_bitcast_fusion
  141.0 1.1 multiply_reduce_fusion.2
  142.8 54.5 %all-gather.2.cloned.1.call-done = bf16[1504,2,256]{2,1,0:T(2,128)(2,1)} async-done(((bf16[94,2,256]{2,1,0:T(2,128)(2,1)}), bf16[1504,2,256]{2,1,0:T(2,128)(2,1)}) %all-gather.2.cloned.1.call-update) | async-done | bytes 1540112 | tf_op jit(solution)/shard_map/all_gather | solution.py:156
  197.3 1.3 broadcast_in_dim.52
  198.7 117.5 %while.40 = (s32[]{:T(128)}, f32[16,2,94,94]{3,2,1,0:T(8,128)}, bf16[1504,2,256]{2,1,0:T(2,128)(2,1)}, bf16[188,1,128]{0,2,1:T(8,128)(2,1)S(1)}, f32[94,2]{0,1:T...) while((s32[]{:T(128)}, f32[16,2,94,94]{3,2,1,0:T(8,128)}, ...), condition=%wide.region_11.12_spmd.clone, body=%wide.region_8.11_spmd.clone.sunk | while | flops 1172045696 | bytes 1180199 | solution.py:99
  198.7 1.0 constant_dynamic-slice_fusion.3
  199.8 4.9 %multiply_reduce_fusion.5 = f32[94,188]{1,0:T(8,128)S(1)} fusion(bf16[94,2,256]{0,1,2:T(2,128)(2,1)S(1)} %copy.64, s32[188]{0:T(256)S(1)} %get-tuple-element.532, bf16[188,128]{0,1:T(8,128)(2,1)S(1)} %bitcast.104), kind=kOutput, calls=%fused_computation.18.clone.1 | convolution fusion | flops 1171838208 | bytes 215824 | tf_op jit(solution)/shard_map/while/body/eval_jaxpr/conv_general_dilated | solution.py:65
  206.0 1.0 constant_dynamic-slice_fusion.3
  207.1 4.9 %multiply_reduce_fusion.5 = f32[94,188]{1,0:T(8,128)S(1)} fusion(bf16[94,2,256]{0,1,2:T(2,128)(2,1)S(1)} %copy.64, s32[188]{0:T(256)S(1)} %get-tuple-element.532, bf16[188,128]{0,1:T(8,128)(2,1)S(1)} %bitcast.104), kind=kOutput, calls=%fused_computation.18.clone.1 | convolution fusion | flops 1171838208 | bytes 215824 | tf_op jit(solution)/shard_map/while/body/eval_jaxpr/conv_general_dilated | solution.py:65
  213.4 1.0 constant_dynamic-slice_fusion.3
  214.5 4.9 %multiply_reduce_fusion.5 = f32[94,188]{1,0:T(8,128)S(1)} fusion(bf16[94,2,256]{0,1,2:T(2,128)(2,1)S(1)} %copy.64, s32[188]{0:T(256)S(1)} %get-tuple-element.532, bf16[188,128]{0,1:T(8,128)(2,1)S(1)} %bitcast.104), kind=kOutput, calls=%fused_computation.18.clone.1 | convolution fusion | flops 1171838208 | bytes 215824 | tf_op jit(solution)/shard_map/while/body/eval_jaxpr/conv_general_dilated | solution.py:65
  220.7 1.0 constant_dynamic-slice_fusion.3
  221.8 4.9 %multiply_reduce_fusion.5 = f32[94,188]{1,0:T(8,128)S(1)} fusion(bf16[94,2,256]{0,1,2:T(2,128)(2,1)S(1)} %copy.64, s32[188]{0:T(256)S(1)} %get-tuple-element.532, bf16[188,128]{0,1:T(8,128)(2,1)S(1)} %bitcast.104), kind=kOutput, calls=%fused_computation.18.clone.1 | convolution fusion | flops 1171838208 | bytes 215824 | tf_op jit(solution)/shard_map/while/body/eval_jaxpr/conv_general_dilated | solution.py:65
  228.0 1.0 constant_dynamic-slice_fusion.3
  229.2 4.9 %multiply_reduce_fusion.5 = f32[94,188]{1,0:T(8,128)S(1)} fusion(bf16[94,2,256]{0,1,2:T(2,128)(2,1)S(1)} %copy.64, s32[188]{0:T(256)S(1)} %get-tuple-element.532, bf16[188,128]{0,1:T(8,128)(2,1)S(1)} %bitcast.104), kind=kOutput, calls=%fused_computation.18.clone.1 | convolution fusion | flops 1171838208 | bytes 215824 | tf_op jit(solution)/shard_map/while/body/eval_jaxpr/conv_general_dilated | solution.py:65
  235.4 1.0 constant_dynamic-slice_fusion.3
  236.5 4.9 %multiply_reduce_fusion.5 = f32[94,188]{1,0:T(8,128)S(1)} fusion(bf16[94,2,256]{0,1,2:T(2,128)(2,1)S(1)} %copy.64, s32[188]{0:T(256)S(1)} %get-tuple-element.532, bf16[188,128]{0,1:T(8,128)(2,1)S(1)} %bitcast.104), kind=kOutput, calls=%fused_computation.18.clone.1 | convolution fusion | flops 1171838208 | bytes 215824 | tf_op jit(solution)/shard_map/while/body/eval_jaxpr/conv_general_dilated | solution.py:65
  242.7 1.0 constant_dynamic-slice_fusion.3
  243.9 4.9 %multiply_reduce_fusion.5 = f32[94,188]{1,0:T(8,128)S(1)} fusion(bf16[94,2,256]{0,1,2:T(2,128)(2,1)S(1)} %copy.64, s32[188]{0:T(256)S(1)} %get-tuple-element.532, bf16[188,128]{0,1:T(8,128)(2,1)S(1)} %bitcast.104), kind=kOutput, calls=%fused_computation.18.clone.1 | convolution fusion | flops 1171838208 | bytes 215824 | tf_op jit(solution)/shard_map/while/body/eval_jaxpr/conv_general_dilated | solution.py:65
  250.1 1.0 constant_dynamic-slice_fusion.3
  251.2 4.9 %multiply_reduce_fusion.5 = f32[94,188]{1,0:T(8,128)S(1)} fusion(bf16[94,2,256]{0,1,2:T(2,128)(2,1)S(1)} %copy.64, s32[188]{0:T(256)S(1)} %get-tuple-element.532, bf16[188,128]{0,1:T(8,128)(2,1)S(1)} %bitcast.104), kind=kOutput, calls=%fused_computation.18.clone.1 | convolution fusion | flops 1171838208 | bytes 215824 | tf_op jit(solution)/shard_map/while/body/eval_jaxpr/conv_general_dilated | solution.py:65
  257.4 1.0 constant_dynamic-slice_fusion.3
  258.6 4.9 %multiply_reduce_fusion.5 = f32[94,188]{1,0:T(8,128)S(1)} fusion(bf16[94,2,256]{0,1,2:T(2,128)(2,1)S(1)} %copy.64, s32[188]{0:T(256)S(1)} %get-tuple-element.532, bf16[188,128]{0,1:T(8,128)(2,1)S(1)} %bitcast.104), kind=kOutput, calls=%fused_computation.18.clone.1 | convolution fusion | flops 1171838208 | bytes 215824 | tf_op jit(solution)/shard_map/while/body/eval_jaxpr/conv_general_dilated | solution.py:65
  265.9 4.9 %multiply_reduce_fusion.5 = f32[94,188]{1,0:T(8,128)S(1)} fusion(bf16[94,2,256]{0,1,2:T(2,128)(2,1)S(1)} %copy.64, s32[188]{0:T(256)S(1)} %get-tuple-element.532, bf16[188,128]{0,1:T(8,128)(2,1)S(1)} %bitcast.104), kind=kOutput, calls=%fused_computation.18.clone.1 | convolution fusion | flops 1171838208 | bytes 215824 | tf_op jit(solution)/shard_map/while/body/eval_jaxpr/conv_general_dilated | solution.py:65
  272.1 1.0 constant_dynamic-slice_fusion.3
  273.3 4.9 %multiply_reduce_fusion.5 = f32[94,188]{1,0:T(8,128)S(1)} fusion(bf16[94,2,256]{0,1,2:T(2,128)(2,1)S(1)} %copy.64, s32[188]{0:T(256)S(1)} %get-tuple-element.532, bf16[188,128]{0,1:T(8,128)(2,1)S(1)} %bitcast.104), kind=kOutput, calls=%fused_computation.18.clone.1 | convolution fusion | flops 1171838208 | bytes 215824 | tf_op jit(solution)/shard_map/while/body/eval_jaxpr/conv_general_dilated | solution.py:65
  280.6 4.9 %multiply_reduce_fusion.5 = f32[94,188]{1,0:T(8,128)S(1)} fusion(bf16[94,2,256]{0,1,2:T(2,128)(2,1)S(1)} %copy.64, s32[188]{0:T(256)S(1)} %get-tuple-element.532, bf16[188,128]{0,1:T(8,128)(2,1)S(1)} %bitcast.104), kind=kOutput, calls=%fused_computation.18.clone.1 | convolution fusion | flops 1171838208 | bytes 215824 | tf_op jit(solution)/shard_map/while/body/eval_jaxpr/conv_general_dilated | solution.py:65
  287.9 4.9 %multiply_reduce_fusion.5 = f32[94,188]{1,0:T(8,128)S(1)} fusion(bf16[94,2,256]{0,1,2:T(2,128)(2,1)S(1)} %copy.64, s32[188]{0:T(256)S(1)} %get-tuple-element.532, bf16[188,128]{0,1:T(8,128)(2,1)S(1)} %bitcast.104), kind=kOutput, calls=%fused_computation.18.clone.1 | convolution fusion | flops 1171838208 | bytes 215824 | tf_op jit(solution)/shard_map/while/body/eval_jaxpr/conv_general_dilated | solution.py:65
  294.2 1.0 constant_dynamic-slice_fusion.3
  295.3 4.9 %multiply_reduce_fusion.5 = f32[94,188]{1,0:T(8,128)S(1)} fusion(bf16[94,2,256]{0,1,2:T(2,128)(2,1)S(1)} %copy.64, s32[188]{0:T(256)S(1)} %get-tuple-element.532, bf16[188,128]{0,1:T(8,128)(2,1)S(1)} %bitcast.104), kind=kOutput, calls=%fused_computation.18.clone.1 | convolution fusion | flops 1171838208 | bytes 215824 | tf_op jit(solution)/shard_map/while/body/eval_jaxpr/conv_general_dilated | solution.py:65
  302.6 4.9 %multiply_reduce_fusion.5 = f32[94,188]{1,0:T(8,128)S(1)} fusion(bf16[94,2,256]{0,1,2:T(2,128)(2,1)S(1)} %copy.64, s32[188]{0:T(256)S(1)} %get-tuple-element.532, bf16[188,128]{0,1:T(8,128)(2,1)S(1)} %bitcast.104), kind=kOutput, calls=%fused_computation.18.clone.1 | convolution fusion | flops 1171838208 | bytes 215824 | tf_op jit(solution)/shard_map/while/body/eval_jaxpr/conv_general_dilated | solution.py:65
  310.0 4.9 %multiply_reduce_fusion.5 = f32[94,188]{1,0:T(8,128)S(1)} fusion(bf16[94,2,256]{0,1,2:T(2,128)(2,1)S(1)} %copy.64, s32[188]{0:T(256)S(1)} %get-tuple-element.532, bf16[188,128]{0,1:T(8,128)(2,1)S(1)} %bitcast.104), kind=kOutput, calls=%fused_computation.18.clone.1 | convolution fusion | flops 1171838208 | bytes 215824 | tf_op jit(solution)/shard_map/while/body/eval_jaxpr/conv_general_dilated | solution.py:65
  316.2 2.3 copy.42
  318.5 2.8 broadcast_in_dim_reshape.3
  (316 shorter events, 61.5 us)
Async XLA Ops:
  6.5 190.8 %all-gather.2.cloned.1.call-start = ((), (), s32[]{:S(2)}) async-start(), calls=%async_computation | async-start | bytes 1636352 | tf_op jit(solution)/shard_map/all_gather | solution.py:156
  8.5 10.6 %collective-permute-start = (bf16[1280,64]{1,0:T(8,128)(2,1)}, bf16[1280,64]{1,0:T(8,128)(2,1)}, u32[]{:S(2)}, u32[]{:S(2)}) collective-permute-start(bf16[1280,64]{1,0:T(8,128)(2,1)} %get-tuple-element.348), channel_id=1, source_target_pairs={{0,1},{1,2},{2,3},{3,4},{4,5},{5,6},{6,7},{7,8},{8,9},{9,10},{10,1... | collective-permute-start | bytes 491528 | tf_op jit(solution)/shard_map/ppermute | solution.py:28
  13.4 9.1 %collective-permute-start.1 = (bf16[1280,64]{1,0:T(8,128)(2,1)S(1)}, bf16[1280,64]{1,0:T(8,128)(2,1)}, u32[]{:S(2)}, u32[]{:S(2)}) collective-permute-start(bf16[1280,64]{1,0:T(8,128)(2,1)S(1)} %get-tuple-element.349), channel_id=1, source_target_pairs={{1,0},{2,1},{3,2},{4,3},{5,4},{6,5},{7,6},{8,7},{9,8},{10,9},{11,1... | collective-permute-start | bytes 491528 | tf_op jit(solution)/shard_map/ppermute | solution.py:30
  17.1 1.1 copy-start.2
  17.2 5.3 %copy-start = (bf16[1280,128]{1,0:T(8,128)(2,1)S(1)}, bf16[1280,128]{1,0:T(8,128)(2,1)}, u32[]{:S(2)}) copy-start(bf16[1280,128]{1,0:T(8,128)(2,1)} %param.11) | copy-start | bytes 983044
  65.3 57.6 %copy-start.3 = (u32[256]{0:T(256)S(1)}, u32[256]{0:T(256)}, u32[]{:S(2)}) copy-start(u32[256]{0:T(256)} %constant.228) | copy-start | bytes 3076
  121.1 3.1 collective-permute-start.4
  124.5 74.1 %copy-start.4 = (s32[188]{0:T(256)S(1)}, s32[188]{0:T(256)}, u32[]{:S(2)}) copy-start(s32[188]{0:T(256)} %constant.197.clone.2) | copy-start | bytes 2260
  124.7 10.2 %collective-permute-start.2 = (f32[94,2,64]{2,1,0:T(2,128)S(1)}, f32[94,2,64]{2,1,0:T(2,128)S(1)}, u32[]{:S(2)}, u32[]{:S(2)}) collective-permute-start(f32[94,2,64]{2,1,0:T(2,128)S(1)} %get-tuple-element.350), channel_id=1, source_target_pairs={{0,1},{1,2},{2,3},{3,4},{4,5},{5,6},{6,7},{7,8},{8,9},{9,10},{10,1... | collective-permute-start | bytes 144392 | tf_op jit(solution)/shard_map/ppermute | solution.py:28
  132.7 5.9 %collective-permute-start.3 = (f32[94,2,64]{2,1,0:T(2,128)S(1)}, f32[94,2,64]{2,1,0:T(2,128)S(1)}, u32[]{:S(2)}, u32[]{:S(2)}) collective-permute-start(f32[94,2,64]{2,1,0:T(2,128)S(1)} %get-tuple-element.351), channel_id=1, source_target_pairs={{1,0},{2,1},{3,2},{4,3},{5,4},{6,5},{7,6},{8,7},{9,8},{10,9},{11,1... | collective-permute-start | bytes 144392 | tf_op jit(solution)/shard_map/ppermute | solution.py:30
  199.8 5.5 %copy-start.1 = (f32[94,2]{0,1:T(2,128)S(1)}, f32[94,2]{0,1:T(2,128)}, u32[]{:S(2)}) copy-start(f32[94,2]{0,1:T(2,128)} %get-tuple-element.524) | copy-start | bytes 2260 | tf_op jit(solution)/shard_map/while
  207.1 5.5 %copy-start.1 = (f32[94,2]{0,1:T(2,128)S(1)}, f32[94,2]{0,1:T(2,128)}, u32[]{:S(2)}) copy-start(f32[94,2]{0,1:T(2,128)} %get-tuple-element.524) | copy-start | bytes 2260 | tf_op jit(solution)/shard_map/while
  214.5 5.5 %copy-start.1 = (f32[94,2]{0,1:T(2,128)S(1)}, f32[94,2]{0,1:T(2,128)}, u32[]{:S(2)}) copy-start(f32[94,2]{0,1:T(2,128)} %get-tuple-element.524) | copy-start | bytes 2260 | tf_op jit(solution)/shard_map/while
  221.8 5.5 %copy-start.1 = (f32[94,2]{0,1:T(2,128)S(1)}, f32[94,2]{0,1:T(2,128)}, u32[]{:S(2)}) copy-start(f32[94,2]{0,1:T(2,128)} %get-tuple-element.524) | copy-start | bytes 2260 | tf_op jit(solution)/shard_map/while
  229.2 5.5 %copy-start.1 = (f32[94,2]{0,1:T(2,128)S(1)}, f32[94,2]{0,1:T(2,128)}, u32[]{:S(2)}) copy-start(f32[94,2]{0,1:T(2,128)} %get-tuple-element.524) | copy-start | bytes 2260 | tf_op jit(solution)/shard_map/while
  236.5 5.5 %copy-start.1 = (f32[94,2]{0,1:T(2,128)S(1)}, f32[94,2]{0,1:T(2,128)}, u32[]{:S(2)}) copy-start(f32[94,2]{0,1:T(2,128)} %get-tuple-element.524) | copy-start | bytes 2260 | tf_op jit(solution)/shard_map/while
  243.9 5.5 %copy-start.1 = (f32[94,2]{0,1:T(2,128)S(1)}, f32[94,2]{0,1:T(2,128)}, u32[]{:S(2)}) copy-start(f32[94,2]{0,1:T(2,128)} %get-tuple-element.524) | copy-start | bytes 2260 | tf_op jit(solution)/shard_map/while
  251.2 5.5 %copy-start.1 = (f32[94,2]{0,1:T(2,128)S(1)}, f32[94,2]{0,1:T(2,128)}, u32[]{:S(2)}) copy-start(f32[94,2]{0,1:T(2,128)} %get-tuple-element.524) | copy-start | bytes 2260 | tf_op jit(solution)/shard_map/while
  258.5 5.5 %copy-start.1 = (f32[94,2]{0,1:T(2,128)S(1)}, f32[94,2]{0,1:T(2,128)}, u32[]{:S(2)}) copy-start(f32[94,2]{0,1:T(2,128)} %get-tuple-element.524) | copy-start | bytes 2260 | tf_op jit(solution)/shard_map/while
  265.9 5.5 %copy-start.1 = (f32[94,2]{0,1:T(2,128)S(1)}, f32[94,2]{0,1:T(2,128)}, u32[]{:S(2)}) copy-start(f32[94,2]{0,1:T(2,128)} %get-tuple-element.524) | copy-start | bytes 2260 | tf_op jit(solution)/shard_map/while
  273.2 5.5 %copy-start.1 = (f32[94,2]{0,1:T(2,128)S(1)}, f32[94,2]{0,1:T(2,128)}, u32[]{:S(2)}) copy-start(f32[94,2]{0,1:T(2,128)} %get-tuple-element.524) | copy-start | bytes 2260 | tf_op jit(solution)/shard_map/while
  280.6 5.5 %copy-start.1 = (f32[94,2]{0,1:T(2,128)S(1)}, f32[94,2]{0,1:T(2,128)}, u32[]{:S(2)}) copy-start(f32[94,2]{0,1:T(2,128)} %get-tuple-element.524) | copy-start | bytes 2260 | tf_op jit(solution)/shard_map/while
  287.9 5.5 %copy-start.1 = (f32[94,2]{0,1:T(2,128)S(1)}, f32[94,2]{0,1:T(2,128)}, u32[]{:S(2)}) copy-start(f32[94,2]{0,1:T(2,128)} %get-tuple-element.524) | copy-start | bytes 2260 | tf_op jit(solution)/shard_map/while
  295.3 5.5 %copy-start.1 = (f32[94,2]{0,1:T(2,128)S(1)}, f32[94,2]{0,1:T(2,128)}, u32[]{:S(2)}) copy-start(f32[94,2]{0,1:T(2,128)} %get-tuple-element.524) | copy-start | bytes 2260 | tf_op jit(solution)/shard_map/while
  302.6 5.5 %copy-start.1 = (f32[94,2]{0,1:T(2,128)S(1)}, f32[94,2]{0,1:T(2,128)}, u32[]{:S(2)}) copy-start(f32[94,2]{0,1:T(2,128)} %get-tuple-element.524) | copy-start | bytes 2260 | tf_op jit(solution)/shard_map/while
  310.0 5.5 %copy-start.1 = (f32[94,2]{0,1:T(2,128)S(1)}, f32[94,2]{0,1:T(2,128)}, u32[]{:S(2)}) copy-start(f32[94,2]{0,1:T(2,128)} %get-tuple-element.524) | copy-start | bytes 2260 | tf_op jit(solution)/shard_map/while
Sparse Core Ops, SparseCore 0:
  139.8 57.4 all-gather.1
where the time goes:
time: 329 us; the launch traced here: 328 us
  matrix products  87.8 us (27%)
  waiting for transfers between devices  61.6 us (19%)
  blocking collectives  55.7 us (17%)
  local copies, waits for them, and re-layouts  52.7 us (16%)
  other arithmetic  24.8 us (8%)
  starting transfers between devices  19 us (6%)
  between operations  14.3 us (4%)
  loops' own time  12.1 us (4%)
    conv_general_dilated x16, matrix products, block_value(): lax.conv_general_dilated(visiting, kernel, (LAG_STEP,), 'VALID', dimensio...  79 us
    unnamed x1, blocking collectives  55.7 us
    all_gather x1, waiting for transfers between devices, local(): lax.all_gather(centered, 'vert', axis=0, tiled=True)  54.5 us
    dynamic_slice x32, local copies, waits for them, and re-layouts, add_block(): visiting = lax.dynamic_slice_in_dim(piece, block_idx * par_dev, par_dev, 0)  17.8 us
    ppermute x2, starting transfers between devices, extended_2(): lax.ppermute(tail, axis, [(i, (i + 1) % count) for i in range(ends)])  12.9 us
    dynamic_update_slice x16, other arithmetic, add_block(): lax.dynamic_update_slice(total, guarded(visiting, first)[None], (slot, ze...  11.8 us
    another operation x1, loops' own time, local(): lax.map(one_block, jnp.arange(par_dev * lax.axis_size('vert') // par_dev,...  11 us
    dynamic_slice x16, local copies, waits for them, and re-layouts, local(): lax.map(one_block, jnp.arange(par_dev * lax.axis_size('vert') // par_dev,...  9.38 us
  transfers between devices with their start and end apart: 6, of which 3 were waited for; matrix products, arithmetic and copies ran while one was open for 2% of the time, Pallas kernels for 0%

commit v1 on v0

--- a/solution.py
+++ b/solution.py
@@ -1,3 +1,4 @@
+import functools
 from functools import partial
 import math
 import jax
@@ -15,6 +16,16 @@
 LAG_STEP = 1
 NLAG = 129
 EPSILON = 1e-05
+
+
+def settle_the_bench(inp, dev_axis):
+    wide_out = lax.all_to_all(
+        jnp.stack([inp] * lax.axis_size(dev_axis)), axis_name=dev_axis, split_axis=0, concat_axis=0
+    )
+    return jnp.concatenate(wide_out, 0)
+
+
+_change_meshes = functools.partial(settle_the_bench, dev_axis="vert")
 
 
 def extended_2(cells, sides, width):
@@ -153,7 +164,7 @@
     own_ext = extended_2(own_env, (("tm", 2),), LAG)
     centered, own_middle, own_spread = centered_rows(own_ext, t_dev)
     fold_rows = make_fold(own_middle, own_spread, owner_start, par_dev, t_dev)
-    blocks = fold_rows(empty, lax.all_gather(centered, "vert", axis=0, tiled=True), jnp.int32(0))
+    blocks = fold_rows(empty, _change_meshes(centered), jnp.int32(0))
     coupling = blocks.transpose(1, 2, 0, 3).reshape(BANDS, par_dev, total_par)
     return coupling[None]
 

time: 329 us -> 311 us (0.945); the launches traced: 328 us -> 306 us
  waiting for transfers between devices: 61.6 us -> 45.7 us
  between operations: 14.3 us -> 0.96 us
  starting transfers between devices: 19 us -> 26.4 us
    all_gather x1 -> x0, waiting for transfers between devices: 54.5 us -> none  [local(): lax.all_gather(centered, 'vert', axis=0, tiled=True)]
    all_to_all x0 -> x1, waiting for transfers between devices: none -> 38.4 us  [settle_the_bench(): lax.all_to_all(jnp.stack([inp] * lax.axis_size(dev_axis)), axis_name=dev_...]
    all_to_all x0 -> x1, starting transfers between devices: none -> 5.1 us  [settle_the_bench(): lax.all_to_all(jnp.stack([inp] * lax.axis_size(dev_axis)), axis_name=dev_...]
where the time goes in v1:
time: 311 us; the launch traced here: 306 us
  matrix products  87.8 us (28%)
  blocking collectives  55.7 us (18%)
  local copies, waits for them, and re-layouts  53.8 us (17%)
  waiting for transfers between devices  45.7 us (15%)
  starting transfers between devices  26.4 us (8%)
  other arithmetic  23.3 us (7%)
  loops' own time  12.1 us (4%)
    conv_general_dilated x16, matrix products, block_value(): lax.conv_general_dilated(visiting, kernel, (LAG_STEP,), 'VALID', dimensio...  79 us
    unnamed x1, blocking collectives  55.7 us
    all_to_all x1, waiting for transfers between devices, settle_the_bench(): lax.all_to_all(jnp.stack([inp] * lax.axis_size(dev_axis)), axis_name=dev_...  38.4 us
    dynamic_slice x32, local copies, waits for them, and re-layouts, add_block(): visiting = lax.dynamic_slice_in_dim(piece, block_idx * par_dev, par_dev, 0)  17.8 us
    ppermute x2, starting transfers between devices, extended_2(): lax.ppermute(tail, axis, [(i, (i + 1) % count) for i in range(ends)])  15.6 us
    dynamic_update_slice x16, other arithmetic, add_block(): lax.dynamic_update_slice(total, guarded(visiting, first)[None], (slot, ze...  11.9 us
    another operation x1, loops' own time, local(): lax.map(one_block, jnp.arange(par_dev * lax.axis_size('vert') // par_dev,...  11 us
    dynamic_slice x16, local copies, waits for them, and re-layouts, local(): lax.map(one_block, jnp.arange(par_dev * lax.axis_size('vert') // par_dev,...  9.38 us
  transfers between devices with their start and end apart: 6, of which 3 were waited for; matrix products, arithmetic and copies ran while one was open for 2% of the time, Pallas kernels for 0%

profile of v1, /device:TPU:1, one launch (start us, length us, event | category | flops | bytes accessed | tf_op | source)
XLA Modules:
  0.0 305.7 jit_solution(13466340684246284900)
XLA Ops:
  0.0 1.9 fusion.27
  2.0 4.9 %collective-permute-start = (bf16[1280,64]{1,0:T(8,128)(2,1)}, bf16[1280,64]{1,0:T(8,128)(2,1)}, u32[]{:S(2)}, u32[]{:S(2)}) collective-permute-start(bf16[1280,64]{1,0:T(8,128)(2,1)} %get-tuple-element.348), channel_id=1, source_target_pairs={{0,1},{1,2},{2,3},{3,4},{4,5},{5,6},{6,7},{7,8},{8,9},{9,10},{10,1... | collective-permute-start | bytes 491528 | tf_op jit(solution)/shard_map/ppermute | solution.py:39
  6.9 2.2 collective-permute-start.1
  12.6 3.4 %collective-permute-done.1 = bf16[1280,64]{1,0:T(8,128)(2,1)} collective-permute-done((bf16[1280,64]{1,0:T(8,128)(2,1)S(1)}, bf16[1280,64]{1,0:T(8,128)(2,1)}, u32[]{:S(2)}, u32[]{:S(2)}) %collective-permute-start.1) | collective-permute-done | bytes 163872 | tf_op jit(solution)/shard_map/ppermute | solution.py:41
  16.0 1.5 pad_maximum_fusion
  17.5 12.1 %while.38 = (s32[]{:T(128)}, bf16[10,128,2,128]{3,2,1,0:T(2,128)(2,1)}, bf16[10,128,256]{2,1,0:T(8,128)(2,1)S(1)}, bf16[256,768]{0,1:T(8,128)(2,1)S(1)}, bf16[2,192,128]{2,1,0:T(8,128)(2,1)S(1)}, /*index=5*/s32[]{:T(128)}) while((s32[]{:T(128)}, bf16[10,128,2,128]{3,2,1,0:T(2,128)(2,1)}, bf16[10,128,256]{2,1,0:T(8,128)(2,1)S(1)}, ...), condition=%wide.region_1.2_spmd, body=%wide.region_0.1_spmd.sunk | while | flops 63143936 | bytes 1540681 | solution.py:140
  29.5 1.2 copy.64
  30.7 27.9 %while.39 = (s32[]{:T(128)}, f32[16,94,256]{2,1,0:T(8,128)S(1)}, s32[3,1280]{1,0:T(4,128)S(1)}, s32[16]{0:T(128)S(1)}, bf16[1280,256]{1,0:T(8,128)(2,1)S(1)}, /*index=5*/s32[]{:T(128)}, s32[1]{0:T(128)}) while((s32[]{:T(128)}, f32[16,94,256]{2,1,0:T(8,128)S(1)}, s32[3,1280]{1,0:T(4,128)S(1)}, s32[16]{0:T(128)S(1)}, ...), condition=%wide.region_4.5_spmd, body=%wide.region_2.4_spmd.sunk | while | flops 62566496 | bytes 1256285 | solution.py:154
  58.8 55.7 %fusion.2 = f32[96,256]{1,0:T(8,128)S(1)} fusion(f32[1504,256]{1,0:T(8,128)S(1)} %reshape.157), kind=kCustom, calls=%all-reduce-scatter | all-reduce-scatter fusion | flops 393217 | bytes 1639424
  114.5 1.5 collective-permute-start.4
  117.8 10.7 %collective-permute-start.2 = (f32[94,2,64]{2,1,0:T(2,128)S(1)}, f32[94,2,64]{2,1,0:T(2,128)S(1)}, u32[]{:S(2)}, u32[]{:S(2)}) collective-permute-start(f32[94,2,64]{2,1,0:T(2,128)S(1)} %get-tuple-element.350), channel_id=1, source_target_pairs={{0,1},{1,2},{2,3},{3,4},{4,5},{5,6},{6,7},{7,8},{8,9},{9,10},{10,1... | collective-permute-start | bytes 144392 | tf_op jit(solution)/shard_map/ppermute | solution.py:39
  128.5 1.9 collective-permute-start.3
  130.6 3.8 %collective-permute-done.3 = f32[94,2,64]{2,1,0:T(2,128)S(1)} collective-permute-done((f32[94,2,64]{2,1,0:T(2,128)S(1)}, f32[94,2,64]{2,1,0:T(2,128)S(1)}, u32[]{:S(2)}, u32[]{:S(2)}) %collective-permute-start.3) | collective-permute-done | bytes 48160 | tf_op jit(solution)/shard_map/ppermute | solution.py:41
  134.8 1.9 stack.2
  136.8 5.1 %all-to-all-start = ((bf16[16,94,2,256]{3,2,1,0:T(2,128)(2,1)}), bf16[16,94,2,256]{3,2,1,0:T(2,128)(2,1)}, u32[]{:S(2)}, u32[]{:S(2)}) async-start(bf16[16,94,2,256]{3,2,1,0:T(2,128)(2,1)} %stack.2), calls=%async_computation | async-start | bytes 3080192 | tf_op jit(solution)/shard_map/all_to_all | solution.py:22
  143.2 38.4 %all-to-all-done = bf16[16,94,2,256]{3,2,1,0:T(2,128)(2,1)} async-done(((bf16[16,94,2,256]{3,2,1,0:T(2,128)(2,1)}), bf16[16,94,2,256]{3,2,1,0:T(2,128)(2,1)}, u32[]{:S(2)}, u32[]{:S(2)}) %all-to-all-start) | async-done | bytes 1540128 | tf_op jit(solution)/shard_map/all_to_all | solution.py:22
  181.6 1.3 broadcast_in_dim.52
  183.0 117.7 %while.40 = (s32[]{:T(128)}, f32[16,2,94,94]{3,2,1,0:T(8,128)}, bf16[1504,2,256]{2,1,0:T(2,128)(2,1)}, bf16[188,1,128]{0,2,1:T(8,128)(2,1)S(1)}, f32[94,2]{0,1:T...) while((s32[]{:T(128)}, f32[16,2,94,94]{3,2,1,0:T(8,128)}, ...), condition=%wide.region_11.12_spmd.clone, body=%wide.region_8.11_spmd.clone.sunk | while | flops 1172045696 | bytes 1180199 | solution.py:110
  183.0 1.0 constant_dynamic-slice_fusion.3
  184.1 4.9 %multiply_reduce_fusion.5 = f32[94,188]{1,0:T(8,128)S(1)} fusion(bf16[94,2,256]{0,1,2:T(2,128)(2,1)S(1)} %copy.70, s32[188]{0:T(256)S(1)} %get-tuple-element.532, bf16[188,128]{0,1:T(8,128)(2,1)S(1)} %bitcast.105), kind=kOutput, calls=%fused_computation.18.clone.1 | convolution fusion | flops 1171838208 | bytes 215824 | tf_op jit(solution)/shard_map/while/body/eval_jaxpr/conv_general_dilated | solution.py:76
  190.3 1.0 constant_dynamic-slice_fusion.3
  191.5 4.9 %multiply_reduce_fusion.5 = f32[94,188]{1,0:T(8,128)S(1)} fusion(bf16[94,2,256]{0,1,2:T(2,128)(2,1)S(1)} %copy.70, s32[188]{0:T(256)S(1)} %get-tuple-element.532, bf16[188,128]{0,1:T(8,128)(2,1)S(1)} %bitcast.105), kind=kOutput, calls=%fused_computation.18.clone.1 | convolution fusion | flops 1171838208 | bytes 215824 | tf_op jit(solution)/shard_map/while/body/eval_jaxpr/conv_general_dilated | solution.py:76
  197.7 1.0 constant_dynamic-slice_fusion.3
  198.8 4.9 %multiply_reduce_fusion.5 = f32[94,188]{1,0:T(8,128)S(1)} fusion(bf16[94,2,256]{0,1,2:T(2,128)(2,1)S(1)} %copy.70, s32[188]{0:T(256)S(1)} %get-tuple-element.532, bf16[188,128]{0,1:T(8,128)(2,1)S(1)} %bitcast.105), kind=kOutput, calls=%fused_computation.18.clone.1 | convolution fusion | flops 1171838208 | bytes 215824 | tf_op jit(solution)/shard_map/while/body/eval_jaxpr/conv_general_dilated | solution.py:76
  205.0 1.0 constant_dynamic-slice_fusion.3
  206.2 4.9 %multiply_reduce_fusion.5 = f32[94,188]{1,0:T(8,128)S(1)} fusion(bf16[94,2,256]{0,1,2:T(2,128)(2,1)S(1)} %copy.70, s32[188]{0:T(256)S(1)} %get-tuple-element.532, bf16[188,128]{0,1:T(8,128)(2,1)S(1)} %bitcast.105), kind=kOutput, calls=%fused_computation.18.clone.1 | convolution fusion | flops 1171838208 | bytes 215824 | tf_op jit(solution)/shard_map/while/body/eval_jaxpr/conv_general_dilated | solution.py:76
  212.4 1.0 constant_dynamic-slice_fusion.3
  213.5 4.9 %multiply_reduce_fusion.5 = f32[94,188]{1,0:T(8,128)S(1)} fusion(bf16[94,2,256]{0,1,2:T(2,128)(2,1)S(1)} %copy.70, s32[188]{0:T(256)S(1)} %get-tuple-element.532, bf16[188,128]{0,1:T(8,128)(2,1)S(1)} %bitcast.105), kind=kOutput, calls=%fused_computation.18.clone.1 | convolution fusion | flops 1171838208 | bytes 215824 | tf_op jit(solution)/shard_map/while/body/eval_jaxpr/conv_general_dilated | solution.py:76
  219.8 1.0 constant_dynamic-slice_fusion.3
  220.9 4.9 %multiply_reduce_fusion.5 = f32[94,188]{1,0:T(8,128)S(1)} fusion(bf16[94,2,256]{0,1,2:T(2,128)(2,1)S(1)} %copy.70, s32[188]{0:T(256)S(1)} %get-tuple-element.532, bf16[188,128]{0,1:T(8,128)(2,1)S(1)} %bitcast.105), kind=kOutput, calls=%fused_computation.18.clone.1 | convolution fusion | flops 1171838208 | bytes 215824 | tf_op jit(solution)/shard_map/while/body/eval_jaxpr/conv_general_dilated | solution.py:76
  227.1 1.0 constant_dynamic-slice_fusion.3
  228.2 4.9 %multiply_reduce_fusion.5 = f32[94,188]{1,0:T(8,128)S(1)} fusion(bf16[94,2,256]{0,1,2:T(2,128)(2,1)S(1)} %copy.70, s32[188]{0:T(256)S(1)} %get-tuple-element.532, bf16[188,128]{0,1:T(8,128)(2,1)S(1)} %bitcast.105), kind=kOutput, calls=%fused_computation.18.clone.1 | convolution fusion | flops 1171838208 | bytes 215824 | tf_op jit(solution)/shard_map/while/body/eval_jaxpr/conv_general_dilated | solution.py:76
  234.5 1.0 constant_dynamic-slice_fusion.3
  235.6 4.9 %multiply_reduce_fusion.5 = f32[94,188]{1,0:T(8,128)S(1)} fusion(bf16[94,2,256]{0,1,2:T(2,128)(2,1)S(1)} %copy.70, s32[188]{0:T(256)S(1)} %get-tuple-element.532, bf16[188,128]{0,1:T(8,128)(2,1)S(1)} %bitcast.105), kind=kOutput, calls=%fused_computation.18.clone.1 | convolution fusion | flops 1171838208 | bytes 215824 | tf_op jit(solution)/shard_map/while/body/eval_jaxpr/conv_general_dilated | solution.py:76
  241.8 1.0 constant_dynamic-slice_fusion.3
  243.0 4.9 %multiply_reduce_fusion.5 = f32[94,188]{1,0:T(8,128)S(1)} fusion(bf16[94,2,256]{0,1,2:T(2,128)(2,1)S(1)} %copy.70, s32[188]{0:T(256)S(1)} %get-tuple-element.532, bf16[188,128]{0,1:T(8,128)(2,1)S(1)} %bitcast.105), kind=kOutput, calls=%fused_computation.18.clone.1 | convolution fusion | flops 1171838208 | bytes 215824 | tf_op jit(solution)/shard_map/while/body/eval_jaxpr/conv_general_dilated | solution.py:76
  249.2 1.0 constant_dynamic-slice_fusion.3
  250.3 4.9 %multiply_reduce_fusion.5 = f32[94,188]{1,0:T(8,128)S(1)} fusion(bf16[94,2,256]{0,1,2:T(2,128)(2,1)S(1)} %copy.70, s32[188]{0:T(256)S(1)} %get-tuple-element.532, bf16[188,128]{0,1:T(8,128)(2,1)S(1)} %bitcast.105), kind=kOutput, calls=%fused_computation.18.clone.1 | convolution fusion | flops 1171838208 | bytes 215824 | tf_op jit(solution)/shard_map/while/body/eval_jaxpr/conv_general_dilated | solution.py:76
  256.5 1.0 constant_dynamic-slice_fusion.3
  257.7 4.9 %multiply_reduce_fusion.5 = f32[94,188]{1,0:T(8,128)S(1)} fusion(bf16[94,2,256]{0,1,2:T(2,128)(2,1)S(1)} %copy.70, s32[188]{0:T(256)S(1)} %get-tuple-element.532, bf16[188,128]{0,1:T(8,128)(2,1)S(1)} %bitcast.105), kind=kOutput, calls=%fused_computation.18.clone.1 | convolution fusion | flops 1171838208 | bytes 215824 | tf_op jit(solution)/shard_map/while/body/eval_jaxpr/conv_general_dilated | solution.py:76
  263.9 1.0 constant_dynamic-slice_fusion.3
  265.0 4.9 %multiply_reduce_fusion.5 = f32[94,188]{1,0:T(8,128)S(1)} fusion(bf16[94,2,256]{0,1,2:T(2,128)(2,1)S(1)} %copy.70, s32[188]{0:T(256)S(1)} %get-tuple-element.532, bf16[188,128]{0,1:T(8,128)(2,1)S(1)} %bitcast.105), kind=kOutput, calls=%fused_computation.18.clone.1 | convolution fusion | flops 1171838208 | bytes 215824 | tf_op jit(solution)/shard_map/while/body/eval_jaxpr/conv_general_dilated | solution.py:76
  272.4 4.9 %multiply_reduce_fusion.5 = f32[94,188]{1,0:T(8,128)S(1)} fusion(bf16[94,2,256]{0,1,2:T(2,128)(2,1)S(1)} %copy.70, s32[188]{0:T(256)S(1)} %get-tuple-element.532, bf16[188,128]{0,1:T(8,128)(2,1)S(1)} %bitcast.105), kind=kOutput, calls=%fused_computation.18.clone.1 | convolution fusion | flops 1171838208 | bytes 215824 | tf_op jit(solution)/shard_map/while/body/eval_jaxpr/conv_general_dilated | solution.py:76
  279.7 4.9 %multiply_reduce_fusion.5 = f32[94,188]{1,0:T(8,128)S(1)} fusion(bf16[94,2,256]{0,1,2:T(2,128)(2,1)S(1)} %copy.70, s32[188]{0:T(256)S(1)} %get-tuple-element.532, bf16[188,128]{0,1:T(8,128)(2,1)S(1)} %bitcast.105), kind=kOutput, calls=%fused_computation.18.clone.1 | convolution fusion | flops 1171838208 | bytes 215824 | tf_op jit(solution)/shard_map/while/body/eval_jaxpr/conv_general_dilated | solution.py:76
  287.1 4.9 %multiply_reduce_fusion.5 = f32[94,188]{1,0:T(8,128)S(1)} fusion(bf16[94,2,256]{0,1,2:T(2,128)(2,1)S(1)} %copy.70, s32[188]{0:T(256)S(1)} %get-tuple-element.532, bf16[188,128]{0,1:T(8,128)(2,1)S(1)} %bitcast.105), kind=kOutput, calls=%fused_computation.18.clone.1 | convolution fusion | flops 1171838208 | bytes 215824 | tf_op jit(solution)/shard_map/while/body/eval_jaxpr/conv_general_dilated | solution.py:76
  294.4 4.9 %multiply_reduce_fusion.5 = f32[94,188]{1,0:T(8,128)S(1)} fusion(bf16[94,2,256]{0,1,2:T(2,128)(2,1)S(1)} %copy.70, s32[188]{0:T(256)S(1)} %get-tuple-element.532, bf16[188,128]{0,1:T(8,128)(2,1)S(1)} %bitcast.105), kind=kOutput, calls=%fused_computation.18.clone.1 | convolution fusion | flops 1171838208 | bytes 215824 | tf_op jit(solution)/shard_map/while/body/eval_jaxpr/conv_general_dilated | solution.py:76
  300.6 2.3 copy.46
  303.0 2.8 broadcast_in_dim_reshape.3
  (316 shorter events, 61.5 us)
Async XLA Ops:
  2.0 10.6 %collective-permute-start = (bf16[1280,64]{1,0:T(8,128)(2,1)}, bf16[1280,64]{1,0:T(8,128)(2,1)}, u32[]{:S(2)}, u32[]{:S(2)}) collective-permute-start(bf16[1280,64]{1,0:T(8,128)(2,1)} %get-tuple-element.348), channel_id=1, source_target_pairs={{0,1},{1,2},{2,3},{3,4},{4,5},{5,6},{6,7},{7,8},{8,9},{9,10},{10,1... | collective-permute-start | bytes 491528 | tf_op jit(solution)/shard_map/ppermute | solution.py:39
  6.9 9.1 %collective-permute-start.1 = (bf16[1280,64]{1,0:T(8,128)(2,1)S(1)}, bf16[1280,64]{1,0:T(8,128)(2,1)}, u32[]{:S(2)}, u32[]{:S(2)}) collective-permute-start(bf16[1280,64]{1,0:T(8,128)(2,1)S(1)} %get-tuple-element.349), channel_id=1, source_target_pairs={{1,0},{2,1},{3,2},{4,3},{5,4},{6,5},{7,6},{8,7},{9,8},{10,9},{11,1... | collective-permute-start | bytes 491528 | tf_op jit(solution)/shard_map/ppermute | solution.py:41
  10.6 1.1 copy-start.2
  10.7 5.3 %copy-start = (bf16[1280,128]{1,0:T(8,128)(2,1)S(1)}, bf16[1280,128]{1,0:T(8,128)(2,1)}, u32[]{:S(2)}) copy-start(bf16[1280,128]{1,0:T(8,128)(2,1)} %param.11) | copy-start | bytes 983044
  58.8 57.2 %copy-start.3 = (u32[256]{0:T(256)S(1)}, u32[256]{0:T(256)}, u32[]{:S(2)}) copy-start(u32[256]{0:T(256)} %constant.228) | copy-start | bytes 3076
  114.5 2.8 collective-permute-start.4
  117.8 12.8 %collective-permute-start.2 = (f32[94,2,64]{2,1,0:T(2,128)S(1)}, f32[94,2,64]{2,1,0:T(2,128)S(1)}, u32[]{:S(2)}, u32[]{:S(2)}) collective-permute-start(f32[94,2,64]{2,1,0:T(2,128)S(1)} %get-tuple-element.350), channel_id=1, source_target_pairs={{0,1},{1,2},{2,3},{3,4},{4,5},{5,6},{6,7},{7,8},{8,9},{9,10},{10,1... | collective-permute-start | bytes 144392 | tf_op jit(solution)/shard_map/ppermute | solution.py:39
  128.5 5.9 %collective-permute-start.3 = (f32[94,2,64]{2,1,0:T(2,128)S(1)}, f32[94,2,64]{2,1,0:T(2,128)S(1)}, u32[]{:S(2)}, u32[]{:S(2)}) collective-permute-start(f32[94,2,64]{2,1,0:T(2,128)S(1)} %get-tuple-element.351), channel_id=1, source_target_pairs={{1,0},{2,1},{3,2},{4,3},{5,4},{6,5},{7,6},{8,7},{9,8},{10,9},{11,1... | collective-permute-start | bytes 144392 | tf_op jit(solution)/shard_map/ppermute | solution.py:41
  136.8 44.8 %all-to-all-start = ((bf16[16,94,2,256]{3,2,1,0:T(2,128)(2,1)}), bf16[16,94,2,256]{3,2,1,0:T(2,128)(2,1)}, u32[]{:S(2)}, u32[]{:S(2)}) async-start(bf16[16,94,2,256]{3,2,1,0:T(2,128)(2,1)} %stack.2), calls=%async_computation | async-start | bytes 3080192 | tf_op jit(solution)/shard_map/all_to_all | solution.py:22
  141.9 41.1 %copy-start.4 = (s32[188]{0:T(256)S(1)}, s32[188]{0:T(256)}, u32[]{:S(2)}) copy-start(s32[188]{0:T(256)} %constant.197.clone.2) | copy-start | bytes 2260
  184.1 5.5 %copy-start.1 = (f32[94,2]{0,1:T(2,128)S(1)}, f32[94,2]{0,1:T(2,128)}, u32[]{:S(2)}) copy-start(f32[94,2]{0,1:T(2,128)} %get-tuple-element.524) | copy-start | bytes 2260 | tf_op jit(solution)/shard_map/while
  191.5 5.5 %copy-start.1 = (f32[94,2]{0,1:T(2,128)S(1)}, f32[94,2]{0,1:T(2,128)}, u32[]{:S(2)}) copy-start(f32[94,2]{0,1:T(2,128)} %get-tuple-element.524) | copy-start | bytes 2260 | tf_op jit(solution)/shard_map/while
  198.8 5.5 %copy-start.1 = (f32[94,2]{0,1:T(2,128)S(1)}, f32[94,2]{0,1:T(2,128)}, u32[]{:S(2)}) copy-start(f32[94,2]{0,1:T(2,128)} %get-tuple-element.524) | copy-start | bytes 2260 | tf_op jit(solution)/shard_map/while
  206.2 5.5 %copy-start.1 = (f32[94,2]{0,1:T(2,128)S(1)}, f32[94,2]{0,1:T(2,128)}, u32[]{:S(2)}) copy-start(f32[94,2]{0,1:T(2,128)} %get-tuple-element.524) | copy-start | bytes 2260 | tf_op jit(solution)/shard_map/while
  213.5 5.5 %copy-start.1 = (f32[94,2]{0,1:T(2,128)S(1)}, f32[94,2]{0,1:T(2,128)}, u32[]{:S(2)}) copy-start(f32[94,2]{0,1:T(2,128)} %get-tuple-element.524) | copy-start | bytes 2260 | tf_op jit(solution)/shard_map/while
  220.9 5.5 %copy-start.1 = (f32[94,2]{0,1:T(2,128)S(1)}, f32[94,2]{0,1:T(2,128)}, u32[]{:S(2)}) copy-start(f32[94,2]{0,1:T(2,128)} %get-tuple-element.524) | copy-start | bytes 2260 | tf_op jit(solution)/shard_map/while
  228.2 5.5 %copy-start.1 = (f32[94,2]{0,1:T(2,128)S(1)}, f32[94,2]{0,1:T(2,128)}, u32[]{:S(2)}) copy-start(f32[94,2]{0,1:T(2,128)} %get-tuple-element.524) | copy-start | bytes 2260 | tf_op jit(solution)/shard_map/while
  235.6 5.5 %copy-start.1 = (f32[94,2]{0,1:T(2,128)S(1)}, f32[94,2]{0,1:T(2,128)}, u32[]{:S(2)}) copy-start(f32[94,2]{0,1:T(2,128)} %get-tuple-element.524) | copy-start | bytes 2260 | tf_op jit(solution)/shard_map/while
  242.9 5.5 %copy-start.1 = (f32[94,2]{0,1:T(2,128)S(1)}, f32[94,2]{0,1:T(2,128)}, u32[]{:S(2)}) copy-start(f32[94,2]{0,1:T(2,128)} %get-tuple-element.524) | copy-start | bytes 2260 | tf_op jit(solution)/shard_map/while
  250.3 5.5 %copy-start.1 = (f32[94,2]{0,1:T(2,128)S(1)}, f32[94,2]{0,1:T(2,128)}, u32[]{:S(2)}) copy-start(f32[94,2]{0,1:T(2,128)} %get-tuple-element.524) | copy-start | bytes 2260 | tf_op jit(solution)/shard_map/while
  257.6 5.5 %copy-start.1 = (f32[94,2]{0,1:T(2,128)S(1)}, f32[94,2]{0,1:T(2,128)}, u32[]{:S(2)}) copy-start(f32[94,2]{0,1:T(2,128)} %get-tuple-element.524) | copy-start | bytes 2260 | tf_op jit(solution)/shard_map/while
  265.0 5.5 %copy-start.1 = (f32[94,2]{0,1:T(2,128)S(1)}, f32[94,2]{0,1:T(2,128)}, u32[]{:S(2)}) copy-start(f32[94,2]{0,1:T(2,128)} %get-tuple-element.524) | copy-start | bytes 2260 | tf_op jit(solution)/shard_map/while
  272.3 5.5 %copy-start.1 = (f32[94,2]{0,1:T(2,128)S(1)}, f32[94,2]{0,1:T(2,128)}, u32[]{:S(2)}) copy-start(f32[94,2]{0,1:T(2,128)} %get-tuple-element.524) | copy-start | bytes 2260 | tf_op jit(solution)/shard_map/while
  279.7 5.5 %copy-start.1 = (f32[94,2]{0,1:T(2,128)S(1)}, f32[94,2]{0,1:T(2,128)}, u32[]{:S(2)}) copy-start(f32[94,2]{0,1:T(2,128)} %get-tuple-element.524) | copy-start | bytes 2260 | tf_op jit(solution)/shard_map/while
  287.1 5.5 %copy-start.1 = (f32[94,2]{0,1:T(2,128)S(1)}, f32[94,2]{0,1:T(2,128)}, u32[]{:S(2)}) copy-start(f32[94,2]{0,1:T(2,128)} %get-tuple-element.524) | copy-start | bytes 2260 | tf_op jit(solution)/shard_map/while
  294.4 5.5 %copy-start.1 = (f32[94,2]{0,1:T(2,128)S(1)}, f32[94,2]{0,1:T(2,128)}, u32[]{:S(2)}) copy-start(f32[94,2]{0,1:T(2,128)} %get-tuple-element.524) | copy-start | bytes 2260 | tf_op jit(solution)/shard_map/while
